TPU v7x, 512 devices: a whole 4x8x8 slice. The times are simulated.
512 devices in a mesh: dp: 4 (over x), ctx: 16 (over y, core), tensor: 8 (over z).
Axes of the slice: x: 4, y: 8, z: 8, core: 2. Of those that a mesh axis runs over, the one named last changes fastest.
Arguments:
- tokens: bfloat16 [8192, 8192], P(('dp', 'tensor'), 'ctx'), parts along dimension 0, may hold values from -6 to 6
- queries: bfloat16 [8192, 8192], P(('dp', 'ctx'), 'tensor'), parts along dimension 0, may hold values from -100 to 100
- key_value_weight: bfloat16 [8192, 2048], P('ctx', 'tensor'), may hold values from -0.0625 to 0.0625
- out_weight: bfloat16 [8192, 8192], P('tensor', 'ctx'), may hold values from -0.0625 to 0.0625
- doc_lengths: int32 [32], P('dp'), parts along dimension 0, may hold values from 1 to 1024, 2048 in all
- block_order: int32 [128], P('dp'), parts along dimension 0, may hold values from 0 to 31, each once
Outputs:
- mixed: bfloat16 [8192, 8192], P(('dp', 'tensor'), 'ctx'), parts along dimension 0
There are 4 independent parts, one for each index of `dp`. A program takes and returns all parts, laid end to end along the dimension named above; an argument that names none is the same for every part. Nothing has to cross between parts.
Inputs may be any that keep to these rules, and one draw needn't show every extreme that they name: `doc_lengths`: the lengths add up to 2048. `block_order`: each of 0 to 31 once.
All inputs are finite; a program needn't handle non-finite values.
Results may differ from a plain program's by a relative error of at most 0.014.
Values may be sent and summed in bfloat16 or wider, within the bound.
No kernel may reach another device: no remote copies, remote signals or barrier semaphores. Data moves between devices by JAX's collectives and lax.ppermute only.
A program may use at most 64 MiB of HBM per device.

v0:
```python
import math
import jax
import jax.numpy as jnp
from jax import lax
from jax.sharding import PartitionSpec as P

HEAD_WIDTH = 128


def doc_index(positions, doc_ends):
    return jnp.sum((doc_ends[None, :] <= positions[:, None]).astype(jnp.int32), axis=1)


def make_attend(query_groups, query_pos, query_doc, doc_ends):
    scale = 1.0 / jnp.sqrt(jnp.float32(HEAD_WIDTH))

    def attend(running, kv_piece, first_row):
        key_count = kv_piece.shape[0]
        key_pos = first_row + jnp.arange(key_count, dtype=jnp.int32)
        key_doc = doc_index(key_pos, doc_ends)
        allowed = (query_doc[:, None] == key_doc[None, :]) & (
            key_pos[None, :] <= query_pos[:, None]
        )

        def update(state_in):
            top_score, total, weighted = state_in
            split_kv = kv_piece.reshape(key_count, query_groups.shape[1], 2, HEAD_WIDTH)
            keys_now = split_kv[:, :, 0, :]
            values_now = split_kv[:, :, 1, :]
            scores = (
                jnp.einsum(
                    "tkgd,nkd->tkgn", query_groups, keys_now, preferred_element_type=jnp.float32
                )
                * scale
            )
            visible = allowed[:, None, None, :]
            piece_top = jnp.max(jnp.where(visible, scores, jnp.float32(-1e30)), axis=-1)
            new_top = jnp.maximum(top_score, piece_top)
            probs = jnp.where(visible, jnp.exp(scores - new_top[..., None]), jnp.float32(0.0))
            rescale = jnp.exp(top_score - new_top)
            total = total * rescale + jnp.sum(probs, axis=-1)
            weighted = weighted * rescale[..., None] + jnp.einsum(
                "tkgn,nkd->tkgd",
                probs.astype(jnp.bfloat16),
                values_now,
                preferred_element_type=jnp.float32,
            )
            return (new_top, total, weighted)

        def unchanged(state_in):
            return state_in

        return lax.cond(jnp.any(allowed), update, unchanged, running)

    return attend


def local(tokens, queries, key_value_weight, out_weight, doc_lengths, block_order):
    ctx_count = lax.axis_size("ctx")
    ctx_rank = lax.axis_index("ctx")
    local_rows = queries.shape[0]
    seq_rows = local_rows * ctx_count
    half_rows = local_rows // 2
    doc_ends = jnp.cumsum(doc_lengths)
    own_blocks = lax.dynamic_slice_in_dim(block_order, 2 * ctx_rank, 2)
    query_pos = jnp.repeat(
        own_blocks, half_rows, total_repeat_length=local_rows
    ) * half_rows + jnp.tile(jnp.arange(half_rows, dtype=jnp.int32), 2)
    query_doc = doc_index(query_pos, doc_ends)
    heads_width = queries.shape[1]
    kv_heads = key_value_weight.shape[1] // (2 * HEAD_WIDTH)
    queries_per_group = heads_width // HEAD_WIDTH // kv_heads
    query_groups = queries.reshape(local_rows, kv_heads, queries_per_group, HEAD_WIDTH)
    attend = make_attend(query_groups, query_pos, query_doc, doc_ends)
    initial = (
        jnp.full((local_rows, kv_heads, queries_per_group), -1e30, jnp.float32),
        jnp.zeros((local_rows, kv_heads, queries_per_group), jnp.float32),
        jnp.zeros((local_rows, kv_heads, queries_per_group, HEAD_WIDTH), jnp.float32),
    )
    partial_kv = jnp.dot(
        lax.all_gather(tokens, "tensor", axis=0, tiled=True),
        key_value_weight,
        preferred_element_type=jnp.float32,
    )
    whole_kv = lax.psum(partial_kv, "ctx").astype(jnp.bfloat16)
    key_step = math.gcd(seq_rows, 512)

    def visit(key_block, running):
        kv_piece = lax.dynamic_slice_in_dim(whole_kv, key_block * key_step, key_step, 0)
        return attend(running, kv_piece, key_block * key_step)

    result = lax.fori_loop(0, seq_rows // key_step, visit, initial)
    top_score, total, weighted = result
    attn = (weighted / total[..., None]).astype(jnp.bfloat16).reshape(local_rows, heads_width)
    partial_out = jnp.dot(
        lax.all_gather(attn, "ctx", axis=0, tiled=True),
        out_weight,
        preferred_element_type=jnp.float32,
    )
    mixed = lax.psum_scatter(
        partial_out.astype(jnp.bfloat16), "tensor", scatter_dimension=0, tiled=True
    )
    return mixed


def solution(mesh):
    in_specs = (
        P(("dp", "tensor"), "ctx"),
        P(("dp", "ctx"), "tensor"),
        P("ctx", "tensor"),
        P("tensor", "ctx"),
        P("dp"),
        P("dp"),
    )
    out_specs = P(("dp", "tensor"), "ctx")
    return jax.shard_map(local, mesh=mesh, in_specs=in_specs, out_specs=out_specs, check_vma=False)
```

profile of v0, /device:TPU:8, one launch (start us, length us, event | category | flops | bytes accessed | tf_op | source)
XLA Modules:
  0.0 245.9 jit_solution(3208315371400769322)
XLA Ops:
  6.5 0.7 all-gather.3.cloned.1.call-update
  7.3 0.8 reduce-window.10
  8.2 1.1 copy.16
  9.6 0.7 dynamic_slice.14
  10.9 1.9 fusion.19
  12.8 45.1 %all-gather.3.cloned.1.call-done = bf16[2048,512]{1,0:T(8,128)(2,1)} async-done(((bf16[256,512]{1,0:T(8,128)(2,1)}), bf16[2048,512]{1,0:T(8,128)(2,1)}) %all-gather.3.cloned.1.call-update) | async-done | bytes 2097168 | tf_op jit(solution)/shard_map/all_gather | solution.py:81
  58.0 2.3 fusion.22
  60.3 55.5 %all-reduce.1 = bf16[2048,256]{1,0:T(8,128)(2,1)} all-reduce(f32[2048,256]{1,0:T(8,128)S(1)} %fusion.22), channel_id=1, replica_groups=mesh['dp'=4,'ctx'=16,'tensor'=8] {'ctx'}, use_global_device_ids=true, to_apply=%region_0.0 | all-reduce | flops 524288 | bytes 3145728 | tf_op jit(solution)/shard_map/psum | solution.py:85
  115.8 1.5 copy.17
  117.4 15.2 %while.19 = (s32[]{:T(128)}, f32[128,1,8]{0,2,1:T(8,128)S(1)}, f32[128,1,8]{0,2,1:T(8,128)S(1)}, f32[128,1,8,128]{0,3,2,1:T(8,128)S(1)}, s32[128]{0:T(128)S(1)},...) while((s32[]{:T(128)}, f32[128,1,8]{0,2,1:T(8,128)S(1)}, ...), condition=%wide.region_10.11_spmd.clone, body=%wide.region_3.10_spmd.clone.sunk | while | flops 274742656 | bytes 8730577 | solution.py:92
  117.5 1.2 multiply_add_fusion.2
  118.8 0.9 fusion.28
  120.3 1.7 conditional.3
  122.1 1.2 multiply_add_fusion.2
  123.4 0.9 fusion.28
  125.1 1.2 multiply_add_fusion.2
  126.4 0.9 fusion.28
  128.0 1.2 multiply_add_fusion.2
  129.4 0.9 fusion.28
  130.9 1.7 conditional.3
  132.6 0.8 divide_convert_fusion
  133.4 54.3 %all-gather.5.cloned.1.call-done = bf16[2048,1024]{0,1:T(8,128)(2,1)} async-done(((bf16[128,1024]{0,1:T(8,128)(2,1)}), bf16[2048,1024]{0,1:T(8,128)(2,1)}) %all-gather.5.cloned.1.call-update) | async-done | bytes 4194320 | tf_op jit(solution)/shard_map/all_gather | solution.py:96
  187.7 5.9 %convolution_convert_fusion = bf16[2048,512]{1,0:T(8,128)(2,1)} fusion(bf16[2048,1024]{0,1:T(8,128)(2,1)} %all-gather.5.cloned.1.call-done, bf16[1024,512]{1,0:T(8,128)(2,1)S(1)} %copy-done), kind=kOutput, calls=%fused_computation.30 | convolution fusion | flops 2148532224 | bytes 7340032 | tf_op jit(solution)/shard_map/dot_general | solution.py:95
  193.6 45.8 %reduce-scatter.2.cloned.1.call-done = bf16[256,512]{1,0:T(8,128)(2,1)} async-done(((bf16[2048,512]{1,0:T(8,128)(2,1)}), bf16[256,512]{1,0:T(8,128)(2,1)}) %reduce-scatter.2.cloned.1.call-update) | async-done | bytes 262160 | tf_op jit(solution)/shard_map/reduce_scatter | solution.py:100
  (49 shorter events, 5.1 us)
Async XLA Ops:
  6.5 181.1 %copy-start = (bf16[1024,512]{1,0:T(8,128)(2,1)S(1)}, bf16[1024,512]{1,0:T(8,128)(2,1)}, u32[]{:S(2)}) copy-start(bf16[1024,512]{1,0:T(8,128)(2,1)} %param.15) | copy-start | bytes 3145732
  6.5 51.5 %all-gather.3.cloned.1.call-start = ((), (), s32[]{:S(2)}) async-start(), calls=%async_computation.1 | async-start | bytes 2359296 | tf_op jit(solution)/shard_map/all_gather | solution.py:81
  7.3 180.4 %all-gather.5.cloned.1.call-start = ((), (), s32[]{:S(2)}) async-start(), calls=%async_computation.2 | async-start | bytes 4456448 | tf_op jit(solution)/shard_map/all_gather | solution.py:96
  115.8 1.6 copy-start.1
  133.3 106.0 %reduce-scatter.2.cloned.1.call-start = ((), (), s32[]{:S(2)}) async-start(), calls=%async_computation.3 | async-start | bytes 2359296 | tf_op jit(solution)/shard_map/reduce_scatter | solution.py:100
Sparse Core Ops, SparseCore 0:
  9.4 48.5 all-gather.2
  133.5 54.1 all-gather.4
  193.7 45.6 reduce-scatter.1
where the time goes:
time: 246 us
  waiting for transfers between devices  146 us (59%)
  blocking collectives  55.5 us (23%)
  other arithmetic  13.2 us (5%)
  between operations  13.2 us (5%)
  matrix products  10.4 us (4%)
  local copies, waits for them, and re-layouts  4.66 us (2%)
  loops' own time  2.91 us (1%)
    psum x1, blocking collectives, local(): whole_kv = lax.psum(partial_kv, 'ctx').astype(jnp.bfloat16)  55.5 us
    all_gather x1, waiting for transfers between devices, local(): lax.all_gather(attn, 'ctx', axis=0, tiled=True)  54.3 us
    reduce_scatter x1, waiting for transfers between devices, local(): lax.psum_scatter(partial_out.astype(jnp.bfloat16), 'tensor', scatter_dime...  45.8 us
    all_gather x1, waiting for transfers between devices, local(): lax.all_gather(tokens, 'tensor', axis=0, tiled=True)  45.1 us
    add x5, other arithmetic, local(): jnp.repeat(own_blocks, half_rows, total_repeat_length=local_rows)  6.79 us
    dot_general x1, matrix products, local(): jnp.dot(lax.all_gather(attn, 'ctx', axis=0, tiled=True), out_weight, pref...  5.9 us
  transfers between devices with their start and end apart: 3, of which 3 were waited for; matrix products, arithmetic and copies ran while one was open for 2% of the time, Pallas kernels for 0%

commit v1 on v0

--- a/solution.py
+++ b/solution.py
@@ -1,3 +1,4 @@
+import functools
 import math
 import jax
 import jax.numpy as jnp
@@ -5,6 +6,39 @@
 from jax.sharding import PartitionSpec as P
 
 HEAD_WIDTH = 128
+
+
+def end_islands_here(u_in, at_axis):
+    u_in = jnp.moveaxis(u_in, 0, at_axis)
+    all_rows = u_in.shape
+    return u_in.reshape(
+        *all_rows[:at_axis], all_rows[at_axis] * all_rows[at_axis + 1], *all_rows[at_axis + 2 :]
+    )
+
+
+def expand_point(arr_in, link_axis, dim_at):
+    nodes = lax.psum(1, axis_name=link_axis)
+    x_now = range(nodes)
+    t_next = map(lambda j: (j, (j + 1) % nodes), x_now)
+    steps_seen = list(t_next)
+    crops = [(d, num) for num, d in steps_seen]
+    u_next, top = ([], [])
+    for pp in range(nodes - 1):
+        if pp % 2 == 0:
+            u_next.append(
+                lax.ppermute(u_next[-1] if u_next else arr_in, axis_name=link_axis, perm=steps_seen)
+            )
+        else:
+            prior = lax.ppermute(top[-1] if top else arr_in, axis_name=link_axis, perm=crops)
+            top.append(prior)
+    reached = jnp.stack([*u_next[::-1], arr_in, *top])
+    now = lax.axis_index(link_axis)
+    reply = now - len(u_next)
+    reached = reached[(jnp.arange(nodes) - reply) % nodes]
+    return end_islands_here(reached, dim_at)
+
+
+fields_close = functools.partial(expand_point, link_axis="ctx", dim_at=0)
 
 
 def doc_index(positions, doc_ends):
@@ -92,11 +126,7 @@
     result = lax.fori_loop(0, seq_rows // key_step, visit, initial)
     top_score, total, weighted = result
     attn = (weighted / total[..., None]).astype(jnp.bfloat16).reshape(local_rows, heads_width)
-    partial_out = jnp.dot(
-        lax.all_gather(attn, "ctx", axis=0, tiled=True),
-        out_weight,
-        preferred_element_type=jnp.float32,
-    )
+    partial_out = jnp.dot(fields_close(attn), out_weight, preferred_element_type=jnp.float32)
     mixed = lax.psum_scatter(
         partial_out.astype(jnp.bfloat16), "tensor", scatter_dimension=0, tiled=True
     )

time: 246 us -> 276 us (1.12)
  the two profiles are of different devices: /device:TPU:8 before, /device:TPU:10 now
where the time goes in v1:
time: 276 us; the launch traced here: 275 us
  waiting for transfers between devices  134 us (49%)
  blocking collectives  55.5 us (20%)
  local copies, waits for them, and re-layouts  28.2 us (10%)
  starting transfers between devices  17.9 us (6%)
  between operations  13.6 us (5%)
  other arithmetic  13.1 us (5%)
  matrix products  10.4 us (4%)
  loops' own time  2.89 us (1%)
    psum x1, blocking collectives, local(): whole_kv = lax.psum(partial_kv, 'ctx').astype(jnp.bfloat16)  55.5 us
    reduce_scatter x1, waiting for transfers between devices, local(): lax.psum_scatter(partial_out.astype(jnp.bfloat16), 'tensor', scatter_dime...  54.3 us
    all_gather x1, waiting for transfers between devices, local(): lax.all_gather(tokens, 'tensor', axis=0, tiled=True)  44.9 us
    ppermute x8, waiting for transfers between devices, expand_point(): lax.ppermute(u_next[-1] if u_next else arr_in, axis_name=link_axis, perm=...  33.5 us
    unnamed x28, local copies, waits for them, and re-layouts  20.3 us
    ppermute x7, starting transfers between devices, expand_point(): lax.ppermute(top[-1] if top else arr_in, axis_name=link_axis, perm=crops)  17.8 us
    add x5, other arithmetic, local(): jnp.repeat(own_blocks, half_rows, total_repeat_length=local_rows)  7.41 us
    dot_general x1, matrix products, local(): jnp.dot(fields_close(attn), out_weight, preferred_element_type=jnp.float32)  5.87 us
  transfers between devices with their start and end apart: 17, of which 11 were waited for; matrix products, arithmetic and copies ran while one was open for 8% of the time, Pallas kernels for 0%

profile of v1, /device:TPU:10, one launch (start us, length us, event | category | flops | bytes accessed | tf_op | source)
XLA Modules:
  0.0 275.2 jit_solution(11481335622086058192)
XLA Ops:
  10.9 2.0 fusion.21
  13.0 44.9 %all-gather.2.cloned.1.call-done = bf16[2048,512]{1,0:T(8,128)(2,1)} async-done(((bf16[256,512]{1,0:T(8,128)(2,1)}), bf16[2048,512]{1,0:T(8,128)(2,1)}) %all-gather.2.cloned.1.call-update) | async-done | bytes 2097168 | tf_op jit(solution)/shard_map/all_gather | solution.py:115
  58.0 2.3 fusion.24
  60.3 55.5 %all-reduce.1 = bf16[2048,256]{1,0:T(8,128)(2,1)} all-reduce(f32[2048,256]{1,0:T(8,128)S(1)} %fusion.24), channel_id=1, replica_groups=mesh['dp'=4,'ctx'=16,'tensor'=8] {'ctx'}, use_global_device_ids=true, to_apply=%region_0.0 | all-reduce | flops 524288 | bytes 3145728 | tf_op jit(solution)/shard_map/psum | solution.py:119
  117.4 15.7 %while.19 = (s32[]{:T(128)}, f32[128,1,8]{0,2,1:T(8,128)S(1)}, f32[128,1,8]{0,2,1:T(8,128)S(1)}, f32[128,1,8,128]{0,3,2,1:T(8,128)S(1)}, s32[128]{0:T(128)S(1)},...) while((s32[]{:T(128)}, f32[128,1,8]{0,2,1:T(8,128)S(1)}, ...), condition=%wide.region_10.11_spmd.clone, body=%wide.region_3.10_spmd.clone.sunk | while | flops 274742656 | bytes 8730577 | solution.py:126
  133.3 5.8 %collective-permute-done = bf16[128,1024]{1,0:T(8,128)(2,1)S(1)} collective-permute-done((bf16[128,1024]{1,0:T(8,128)(2,1)S(1)}, bf16[128,1024]{1,0:T(8,128)(2,1)S(1)}, u32[]{:S(2)}, u32[]{:S(2)}) %collective-permute-start) | collective-permute-done | bytes 262176 | tf_op jit(solution)/shard_map/ppermute | solution.py:29
  139.0 1.7 collective-permute-start.8
  140.8 4.1 %collective-permute-done.1 = bf16[128,1024]{1,0:T(8,128)(2,1)S(1)} collective-permute-done((bf16[128,1024]{1,0:T(8,128)(2,1)S(1)}, bf16[128,1024]{1,0:T(8,128)(2,1)S(1)}, u32[]{:S(2)}, u32[]{:S(2)}) %collective-permute-start.1) | collective-permute-done | bytes 262176 | tf_op jit(solution)/shard_map/ppermute | solution.py:29
  144.8 1.7 collective-permute-start.9
  146.6 4.0 %collective-permute-done.2 = bf16[128,1024]{1,0:T(8,128)(2,1)S(1)} collective-permute-done((bf16[128,1024]{1,0:T(8,128)(2,1)S(1)}, bf16[128,1024]{1,0:T(8,128)(2,1)S(1)}, u32[]{:S(2)}, u32[]{:S(2)}) %collective-permute-start.2) | collective-permute-done | bytes 262176 | tf_op jit(solution)/shard_map/ppermute | solution.py:29
  150.6 1.9 collective-permute-start.10
  152.6 3.9 %collective-permute-done.3 = bf16[128,1024]{1,0:T(8,128)(2,1)S(1)} collective-permute-done((bf16[128,1024]{1,0:T(8,128)(2,1)S(1)}, bf16[128,1024]{1,0:T(8,128)(2,1)S(1)}, u32[]{:S(2)}, u32[]{:S(2)}) %collective-permute-start.3) | collective-permute-done | bytes 262176 | tf_op jit(solution)/shard_map/ppermute | solution.py:29
  156.5 3.1 %collective-permute-start.11 = (bf16[128,1024]{1,0:T(8,128)(2,1)S(1)}, bf16[128,1024]{1,0:T(8,128)(2,1)S(1)}, u32[]{:S(2)}, u32[]{:S(2)}) collective-permute-start(bf16[128,1024]{1,0:T(8,128)(2,1)S(1)} %collective-permute-done.10), channel_id=1, source_target_pairs={{8,0},{16,8},{24,16},{32,24},{40,32},{48,40},{56,48},{64,56},{72,6... | collective-permute-start | bytes 786440 | tf_op jit(solution)/shard_map/ppermute | solution.py:32
  159.6 3.9 %collective-permute-done.4 = bf16[128,1024]{1,0:T(8,128)(2,1)S(1)} collective-permute-done((bf16[128,1024]{1,0:T(8,128)(2,1)S(1)}, bf16[128,1024]{1,0:T(8,128)(2,1)S(1)}, u32[]{:S(2)}, u32[]{:S(2)}) %collective-permute-start.4) | collective-permute-done | bytes 262176 | tf_op jit(solution)/shard_map/ppermute | solution.py:29
  163.5 3.1 %collective-permute-start.12 = (bf16[128,1024]{1,0:T(8,128)(2,1)S(1)}, bf16[128,1024]{1,0:T(8,128)(2,1)}, u32[]{:S(2)}, u32[]{:S(2)}) collective-permute-start(bf16[128,1024]{1,0:T(8,128)(2,1)S(1)} %collective-permute-done.11), channel_id=1, source_target_pairs={{8,0},{16,8},{24,16},{32,24},{40,32},{48,40},{56,48},{64,56},{72,6... | collective-permute-start | bytes 786440 | tf_op jit(solution)/shard_map/ppermute | solution.py:32
  166.6 3.9 %collective-permute-done.5 = bf16[128,1024]{1,0:T(8,128)(2,1)S(1)} collective-permute-done((bf16[128,1024]{1,0:T(8,128)(2,1)S(1)}, bf16[128,1024]{1,0:T(8,128)(2,1)S(1)}, u32[]{:S(2)}, u32[]{:S(2)}) %collective-permute-start.5) | collective-permute-done | bytes 262176 | tf_op jit(solution)/shard_map/ppermute | solution.py:29
  170.5 3.2 %collective-permute-start.13 = (bf16[128,1024]{1,0:T(8,128)(2,1)}, bf16[128,1024]{1,0:T(8,128)(2,1)}, u32[]{:S(2)}, u32[]{:S(2)}) collective-permute-start(bf16[128,1024]{1,0:T(8,128)(2,1)} %collective-permute-done.12), channel_id=1, source_target_pairs={{8,0},{16,8},{24,16},{32,24},{40,32},{48,40},{56,48},{64,56},{72,6... | collective-permute-start | bytes 786440 | tf_op jit(solution)/shard_map/ppermute | solution.py:32
  173.8 3.9 %collective-permute-done.6 = bf16[128,1024]{1,0:T(8,128)(2,1)} collective-permute-done((bf16[128,1024]{1,0:T(8,128)(2,1)S(1)}, bf16[128,1024]{1,0:T(8,128)(2,1)}, u32[]{:S(2)}, u32[]{:S(2)}) %collective-permute-start.6) | collective-permute-done | bytes 262176 | tf_op jit(solution)/shard_map/ppermute | solution.py:29
  178.0 3.0 %collective-permute-start.14 = (bf16[128,1024]{1,0:T(8,128)(2,1)}, bf16[128,1024]{1,0:T(8,128)(2,1)S(1)}, u32[]{:S(2)}, u32[]{:S(2)}) collective-permute-start(bf16[128,1024]{1,0:T(8,128)(2,1)} %collective-permute-done.13), channel_id=1, source_target_pairs={{8,0},{16,8},{24,16},{32,24},{40,32},{48,40},{56,48},{64,56},{72,6... | collective-permute-start | bytes 786440 | tf_op jit(solution)/shard_map/ppermute | solution.py:32
  181.0 4.0 %collective-permute-done.7 = bf16[128,1024]{1,0:T(8,128)(2,1)} collective-permute-done((bf16[128,1024]{1,0:T(8,128)(2,1)}, bf16[128,1024]{1,0:T(8,128)(2,1)}, u32[]{:S(2)}, u32[]{:S(2)}) %collective-permute-start.7) | collective-permute-done | bytes 262176 | tf_op jit(solution)/shard_map/ppermute | solution.py:29
  200.8 1.7 bitcast_dynamic-update-slice_fusion.1
  203.2 5.0 %gather_fusion = bf16[16,128,1024]{2,1,0:T(8,128)(2,1)} fusion(bf16[16,128,1024]{2,1,0:T(8,128)(2,1)} %bitcast_dynamic-update-slice_fusion, s32[1024]{0:T(1024)S(1)} %pad_clamp_fusion), kind=kCustom, calls=%fused_computation | custom fusion | bytes 8388672 | tf_op jit(solution)/shard_map/gather | solution.py:37
  208.2 5.9 %convolution_convert_fusion = bf16[2048,512]{1,0:T(8,128)(2,1)} fusion(bf16[2048,1024]{1,0:T(8,128)(2,1)} %bitcast.101, bf16[1024,512]{1,0:T(8,128)(2,1)S(1)} %copy-done), kind=kOutput, calls=%fused_computation.31 | convolution fusion | flops 2148532224 | bytes 7340032 | tf_op jit(solution)/shard_map/dot_general | solution.py:129
  214.0 54.3 %reduce-scatter.2.cloned.1.call-done = bf16[256,512]{1,0:T(8,128)(2,1)} async-done(((bf16[2048,512]{1,0:T(8,128)(2,1)}), bf16[256,512]{1,0:T(8,128)(2,1)}) %reduce-scatter.2.cloned.1.call-update) | async-done | bytes 262160 | tf_op jit(solution)/shard_map/reduce_scatter | solution.py:130
  (103 shorter events, 39.2 us)
Async XLA Ops:
  6.5 201.6 %copy-start = (bf16[1024,512]{1,0:T(8,128)(2,1)S(1)}, bf16[1024,512]{1,0:T(8,128)(2,1)}, u32[]{:S(2)}) copy-start(bf16[1024,512]{1,0:T(8,128)(2,1)} %param.15) | copy-start | bytes 3145732
  6.5 51.4 %all-gather.2.cloned.1.call-start = ((), (), s32[]{:S(2)}) async-start(), calls=%async_computation.1 | async-start | bytes 2359296 | tf_op jit(solution)/shard_map/all_gather | solution.py:115
  7.3 261.1 %reduce-scatter.2.cloned.1.call-start = ((), (), s32[]{:S(2)}) async-start(), calls=%async_computation.2 | async-start | bytes 2359296 | tf_op jit(solution)/shard_map/reduce_scatter | solution.py:130
  60.3 57.1 %copy-start.4 = (pred[128]{0:T(512)(128)(4,1)S(1)}, pred[128]{0:T(512)(128)(4,1)}, u32[]{:S(2)}) copy-start(pred[128]{0:T(512)(128)(4,1)} %constant.181) | copy-start | bytes 388
  133.2 5.8 %collective-permute-start = (bf16[128,1024]{1,0:T(8,128)(2,1)S(1)}, bf16[128,1024]{1,0:T(8,128)(2,1)S(1)}, u32[]{:S(2)}, u32[]{:S(2)}) collective-permute-start(bf16[128,1024]{1,0:T(8,128)(2,1)S(1)} %copy.29), channel_id=1, source_target_pairs={{0,8},{8,16},{16,24},{24,32},{32,40},{40,48},{48,56},{56,64},{64,7... | collective-permute-start | bytes 786440 | tf_op jit(solution)/shard_map/ppermute | solution.py:29
  139.0 5.8 %collective-permute-start.1 = (bf16[128,1024]{1,0:T(8,128)(2,1)S(1)}, bf16[128,1024]{1,0:T(8,128)(2,1)S(1)}, u32[]{:S(2)}, u32[]{:S(2)}) collective-permute-start(bf16[128,1024]{1,0:T(8,128)(2,1)S(1)} %collective-permute-done), channel_id=1, source_target_pairs={{0,8},{8,16},{16,24},{24,32},{32,40},{40,48},{48,56},{56,64},{64,7... | collective-permute-start | bytes 786440 | tf_op jit(solution)/shard_map/ppermute | solution.py:29
  139.0 5.8 %collective-permute-start.8 = (bf16[128,1024]{1,0:T(8,128)(2,1)S(1)}, bf16[128,1024]{1,0:T(8,128)(2,1)S(1)}, u32[]{:S(2)}, u32[]{:S(2)}) collective-permute-start(bf16[128,1024]{1,0:T(8,128)(2,1)S(1)} %copy.29), channel_id=1, source_target_pairs={{8,0},{16,8},{24,16},{32,24},{40,32},{48,40},{56,48},{64,56},{72,6... | collective-permute-start | bytes 786440 | tf_op jit(solution)/shard_map/ppermute | solution.py:32
  144.8 5.8 %collective-permute-start.2 = (bf16[128,1024]{1,0:T(8,128)(2,1)S(1)}, bf16[128,1024]{1,0:T(8,128)(2,1)S(1)}, u32[]{:S(2)}, u32[]{:S(2)}) collective-permute-start(bf16[128,1024]{1,0:T(8,128)(2,1)S(1)} %collective-permute-done.1), channel_id=1, source_target_pairs={{0,8},{8,16},{16,24},{24,32},{32,40},{40,48},{48,56},{56,64},{64,7... | collective-permute-start | bytes 786440 | tf_op jit(solution)/shard_map/ppermute | solution.py:29
  144.8 5.8 %collective-permute-start.9 = (bf16[128,1024]{1,0:T(8,128)(2,1)S(1)}, bf16[128,1024]{1,0:T(8,128)(2,1)S(1)}, u32[]{:S(2)}, u32[]{:S(2)}) collective-permute-start(bf16[128,1024]{1,0:T(8,128)(2,1)S(1)} %collective-permute-done.8), channel_id=1, source_target_pairs={{8,0},{16,8},{24,16},{32,24},{40,32},{48,40},{56,48},{64,56},{72,6... | collective-permute-start | bytes 786440 | tf_op jit(solution)/shard_map/ppermute | solution.py:32
  150.6 5.9 %collective-permute-start.3 = (bf16[128,1024]{1,0:T(8,128)(2,1)S(1)}, bf16[128,1024]{1,0:T(8,128)(2,1)S(1)}, u32[]{:S(2)}, u32[]{:S(2)}) collective-permute-start(bf16[128,1024]{1,0:T(8,128)(2,1)S(1)} %collective-permute-done.2), channel_id=1, source_target_pairs={{0,8},{8,16},{16,24},{24,32},{32,40},{40,48},{48,56},{56,64},{64,7... | collective-permute-start | bytes 786440 | tf_op jit(solution)/shard_map/ppermute | solution.py:29
  150.6 5.9 %collective-permute-start.10 = (bf16[128,1024]{1,0:T(8,128)(2,1)S(1)}, bf16[128,1024]{1,0:T(8,128)(2,1)S(1)}, u32[]{:S(2)}, u32[]{:S(2)}) collective-permute-start(bf16[128,1024]{1,0:T(8,128)(2,1)S(1)} %collective-permute-done.9), channel_id=1, source_target_pairs={{8,0},{16,8},{24,16},{32,24},{40,32},{48,40},{56,48},{64,56},{72,6... | collective-permute-start | bytes 786440 | tf_op jit(solution)/shard_map/ppermute | solution.py:32
  156.5 14.0 %copy-start.1 = (bf16[128,1024]{1,0:T(8,128)(2,1)}, bf16[128,1024]{1,0:T(8,128)(2,1)S(1)}, u32[]{:S(2)}) copy-start(bf16[128,1024]{1,0:T(8,128)(2,1)S(1)} %collective-permute-done.3) | copy-start | bytes 786436
  156.5 7.0 %collective-permute-start.4 = (bf16[128,1024]{1,0:T(8,128)(2,1)S(1)}, bf16[128,1024]{1,0:T(8,128)(2,1)S(1)}, u32[]{:S(2)}, u32[]{:S(2)}) collective-permute-start(bf16[128,1024]{1,0:T(8,128)(2,1)S(1)} %collective-permute-done.3), channel_id=1, source_target_pairs={{0,8},{8,16},{16,24},{24,32},{32,40},{40,48},{48,56},{56,64},{64,7... | collective-permute-start | bytes 786440 | tf_op jit(solution)/shard_map/ppermute | solution.py:29
  156.5 7.0 %collective-permute-start.11 = (bf16[128,1024]{1,0:T(8,128)(2,1)S(1)}, bf16[128,1024]{1,0:T(8,128)(2,1)S(1)}, u32[]{:S(2)}, u32[]{:S(2)}) collective-permute-start(bf16[128,1024]{1,0:T(8,128)(2,1)S(1)} %collective-permute-done.10), channel_id=1, source_target_pairs={{8,0},{16,8},{24,16},{32,24},{40,32},{48,40},{56,48},{64,56},{72,6... | collective-permute-start | bytes 786440 | tf_op jit(solution)/shard_map/ppermute | solution.py:32
  163.5 10.3 %copy-start.2 = (bf16[128,1024]{1,0:T(8,128)(2,1)}, bf16[128,1024]{1,0:T(8,128)(2,1)S(1)}, u32[]{:S(2)}) copy-start(bf16[128,1024]{1,0:T(8,128)(2,1)S(1)} %collective-permute-done.4) | copy-start | bytes 786436
  163.5 7.0 %collective-permute-start.5 = (bf16[128,1024]{1,0:T(8,128)(2,1)S(1)}, bf16[128,1024]{1,0:T(8,128)(2,1)S(1)}, u32[]{:S(2)}, u32[]{:S(2)}) collective-permute-start(bf16[128,1024]{1,0:T(8,128)(2,1)S(1)} %collective-permute-done.4), channel_id=1, source_target_pairs={{0,8},{8,16},{16,24},{24,32},{32,40},{40,48},{48,56},{56,64},{64,7... | collective-permute-start | bytes 786440 | tf_op jit(solution)/shard_map/ppermute | solution.py:29
  163.5 7.0 %collective-permute-start.12 = (bf16[128,1024]{1,0:T(8,128)(2,1)S(1)}, bf16[128,1024]{1,0:T(8,128)(2,1)}, u32[]{:S(2)}, u32[]{:S(2)}) collective-permute-start(bf16[128,1024]{1,0:T(8,128)(2,1)S(1)} %collective-permute-done.11), channel_id=1, source_target_pairs={{8,0},{16,8},{24,16},{32,24},{40,32},{48,40},{56,48},{64,56},{72,6... | collective-permute-start | bytes 786440 | tf_op jit(solution)/shard_map/ppermute | solution.py:32
  170.5 7.1 %copy-start.3 = (bf16[128,1024]{1,0:T(8,128)(2,1)}, bf16[128,1024]{1,0:T(8,128)(2,1)S(1)}, u32[]{:S(2)}) copy-start(bf16[128,1024]{1,0:T(8,128)(2,1)S(1)} %collective-permute-done.5) | copy-start | bytes 786436
  170.5 7.1 %collective-permute-start.6 = (bf16[128,1024]{1,0:T(8,128)(2,1)S(1)}, bf16[128,1024]{1,0:T(8,128)(2,1)}, u32[]{:S(2)}, u32[]{:S(2)}) collective-permute-start(bf16[128,1024]{1,0:T(8,128)(2,1)S(1)} %collective-permute-done.5), channel_id=1, source_target_pairs={{0,8},{8,16},{16,24},{24,32},{32,40},{40,48},{48,56},{56,64},{64,7... | collective-permute-start | bytes 786440 | tf_op jit(solution)/shard_map/ppermute | solution.py:29
  170.5 7.4 %collective-permute-start.13 = (bf16[128,1024]{1,0:T(8,128)(2,1)}, bf16[128,1024]{1,0:T(8,128)(2,1)}, u32[]{:S(2)}, u32[]{:S(2)}) collective-permute-start(bf16[128,1024]{1,0:T(8,128)(2,1)} %collective-permute-done.12), channel_id=1, source_target_pairs={{8,0},{16,8},{24,16},{32,24},{40,32},{48,40},{56,48},{64,56},{72,6... | collective-permute-start | bytes 786440 | tf_op jit(solution)/shard_map/ppermute | solution.py:32
  177.6 7.4 %collective-permute-start.7 = (bf16[128,1024]{1,0:T(8,128)(2,1)}, bf16[128,1024]{1,0:T(8,128)(2,1)}, u32[]{:S(2)}, u32[]{:S(2)}) collective-permute-start(bf16[128,1024]{1,0:T(8,128)(2,1)} %collective-permute-done.6), channel_id=1, source_target_pairs={{0,8},{8,16},{16,24},{24,32},{32,40},{40,48},{48,56},{56,64},{64,7... | collective-permute-start | bytes 786440 | tf_op jit(solution)/shard_map/ppermute | solution.py:29
  178.0 24.5 %collective-permute-start.14 = (bf16[128,1024]{1,0:T(8,128)(2,1)}, bf16[128,1024]{1,0:T(8,128)(2,1)S(1)}, u32[]{:S(2)}, u32[]{:S(2)}) collective-permute-start(bf16[128,1024]{1,0:T(8,128)(2,1)} %collective-permute-done.13), channel_id=1, source_target_pairs={{8,0},{16,8},{24,16},{32,24},{40,32},{48,40},{56,48},{64,56},{72,6... | collective-permute-start | bytes 786440 | tf_op jit(solution)/shard_map/ppermute | solution.py:32
Sparse Core Ops, SparseCore 0:
  9.4 48.5 all-gather.1
  214.2 54.1 reduce-scatter.1
